TPU v7x, 128 devices: a whole 4x4x4 slice. The times are simulated.
128 devices in a mesh: dp: 8 (over z_hi, y), ty: 4 (over z_lo, core), tz: 4 (over x).
Axes of the slice: x: 4, y: 4, z: 4 (z_hi: 2, z_lo: 2; z = z_hi * 2 + z_lo), core: 2. Of those that a mesh axis runs over, the one named last changes fastest.
Arguments:
- inputs: bfloat16 [8, 4, 48, 48, 256], P('dp', None, 'ty', 'tz'), may hold values from -6 to 6
- pre_first: bfloat16 [8, 4, 48, 48, 256], P('dp', None, 'ty', 'tz'), may hold values from -6 to 6
- pre_second: bfloat16 [8, 4, 48, 48, 256], P('dp', None, 'ty', 'tz'), may hold values from -6 to 6
- grad_out: bfloat16 [8, 4, 48, 48, 256], P('dp', None, 'ty', 'tz'), may hold values from -6 to 6
- w_first: bfloat16 [256, 27, 256], P('dp'), may hold values from -0.078125 to 0.078125
- w_second: bfloat16 [256, 27, 256], P('dp'), may hold values from -0.078125 to 0.078125
Outputs:
- grad_input: bfloat16 [8, 4, 48, 48, 256], P('dp', None, 'ty', 'tz')
- grad_w_first: float32 [256, 27, 256], P('dp')
- grad_w_second: float32 [256, 27, 256], P('dp')
All inputs are finite; a program needn't handle non-finite values.
Results may differ from a plain program's by a relative error of at most 0.0049.
Values may be sent and summed in bfloat16 or wider, within the bound.
No kernel may reach another device: no remote copies, remote signals or barrier semaphores. Data moves between devices by JAX's collectives and lax.ppermute only.
A program may use at most 128 MiB of HBM per device.

v0:
```python
import math
import jax
import jax.numpy as jnp
from jax import lax
from jax.sharding import PartitionSpec as P


def extended(block, sides, width):
    for axis, dim in sides:
        count = lax.axis_size(axis)
        forward = [(i, i + 1) for i in range(count - 1)]
        backward = [(target, source) for source, target in forward]
        low = lax.ppermute(
            lax.slice_in_dim(block, block.shape[dim] - width, None, axis=dim), axis, forward
        )
        high = lax.ppermute(lax.slice_in_dim(block, 0, width, axis=dim), axis, backward)
        block = jnp.concatenate([low, block, high], axis=dim)
    return block


def make_offsets():
    return [
        (shift_a, shift_b, shift_c)
        for shift_a in (-1, 0, 1)
        for shift_b in (-1, 0, 1)
        for shift_c in (-1, 0, 1)
    ]


def pad_depth(field):
    return jnp.pad(field, ((0, 0), (1, 1), (0, 0), (0, 0), (0, 0)))


def window(padded, offset, shape):
    return padded[
        :,
        1 + offset[0] : 1 + offset[0] + shape[1],
        1 + offset[1] : 1 + offset[1] + shape[2],
        1 + offset[2] : 1 + offset[2] + shape[3],
        :,
    ]


def transpose_maker(grad_pad, shape, piece):
    total = jnp.zeros((shape[0] * shape[1] * shape[2] * shape[3], piece.shape[0]), jnp.float32)
    for index, offset in enumerate(make_offsets()):
        back = (-offset[0], -offset[1], -offset[2])
        sliced = window(grad_pad, back, shape).reshape(-1, grad_pad.shape[4])
        total = total + lax.dot_general(
            sliced, piece[:, index, :], (((1,), (1,)), ((), ())), preferred_element_type=jnp.float32
        )
    return total.reshape(shape[0], shape[1], shape[2], shape[3], piece.shape[0])


def filter_from_inputs(act_pad, grad, shape):
    flat_grad = grad.reshape(-1, grad.shape[4])
    terms = []
    for index, offset in enumerate(make_offsets()):
        sliced = window(act_pad, offset, shape).reshape(-1, act_pad.shape[4])
        terms.append(
            lax.dot_general(
                sliced, flat_grad, (((0,), (0,)), ((), ())), preferred_element_type=jnp.float32
            )
        )
    return jnp.stack(terms, axis=1)


def reduce_terms(partial_value):
    ch_in, tap_count, ch_out = partial_value.shape
    flat = partial_value.reshape(ch_in * tap_count, ch_out)
    share = lax.psum_scatter(flat, ("dp", "ty", "tz"), scatter_dimension=0, tiled=True)
    whole = lax.all_gather(share, ("ty", "tz"), axis=0, tiled=True)
    return whole.reshape(-1, tap_count, ch_out)


def local(inputs, pre_first, pre_second, grad_out, w_first, w_second):
    shape = grad_out.shape
    count = (
        shape[0]
        * shape[1]
        * shape[2]
        * shape[3]
        * lax.axis_size("dp")
        * lax.axis_size("ty")
        * lax.axis_size("tz")
    )
    scale = 1.0 / math.sqrt(count)
    zero_half = jnp.zeros((), jnp.bfloat16)
    grad_top = jnp.where(pre_second > 0, grad_out, zero_half)
    active = jnp.where(pre_first > 0, pre_first, zero_half)
    top_pad = pad_depth(extended(grad_top, (("ty", 2), ("tz", 3)), 1))
    upstream = transpose_maker(top_pad, shape, lax.all_gather(w_second, "dp", axis=0, tiled=True))
    grad_low = jnp.where(pre_first > 0, upstream, jnp.zeros((), jnp.float32)).astype(jnp.bfloat16)
    low_pad = pad_depth(extended(grad_low, (("ty", 2), ("tz", 3)), 1))
    input_pad, active_pad = (
        extended(inputs, (("ty", 2), ("tz", 3)), 1),
        extended(active, (("ty", 2), ("tz", 3)), 1),
    )
    part_second = filter_from_inputs(pad_depth(active_pad), grad_top, shape)
    part_first = filter_from_inputs(pad_depth(input_pad), grad_low, shape)
    grad_w_second = reduce_terms(part_second * scale)
    grad_input = transpose_maker(
        low_pad, shape, lax.all_gather(w_first, "dp", axis=0, tiled=True)
    ).astype(jnp.bfloat16)
    grad_w_first = reduce_terms(part_first * scale)
    return (grad_input, grad_w_first, grad_w_second)


def solution(mesh):
    placed = (
        P("dp", None, "ty", "tz", None),
        P("dp", None, "ty", "tz", None),
        P("dp", None, "ty", "tz", None),
        P("dp", None, "ty", "tz", None),
        P("dp", None, None),
        P("dp", None, None),
    )
    return jax.shard_map(
        local,
        mesh=mesh,
        in_specs=placed,
        out_specs=(P("dp", None, "ty", "tz", None), P("dp", None, None), P("dp", None, None)),
        check_vma=False,
    )
```

profile of v0, /device:TPU:82, one launch (start us, length us, event | category | flops | bytes accessed | tf_op | source)
XLA Modules:
  0.0 719.6 jit_solution(10167780539327095880)
XLA Ops:
  13.9 4.4 collective-permute-start.8
  20.6 3.4 collective-permute-start.2
  24.0 2.4 collective-permute-start.3
  31.3 3.4 collective-permute-start.10
  34.7 3.0 collective-permute-start.11
  39.4 2.4 fusion.181
  94.2 3.2 collective-permute-start.12
  114.7 3.4 broadcast_multiply_fusion.1
  118.9 10.7 %copy.44 = f32[256,27,256]{2,1,0:T(8,128)} copy(f32[256,27,256]{2,0,1:T(8,128)} %broadcast_multiply_fusion.1) | data formatting | bytes 14155776 | tf_op jit(solution)/shard_map/mul | solution.py:105
  129.6 8.5 %mul.15 = f32[6912,256]{1,0:T(8,128)} reshape(f32[256,27,256]{2,1,0:T(8,128)} %copy.44) | data formatting | bytes 14155776 | tf_op jit(solution)/shard_map/mul | solution.py:105
  138.1 5.2 collective-permute-start.4
  144.8 2.9 collective-permute-start.14
  147.7 3.0 collective-permute-start.15
  152.3 2.9 collective-permute-start.6
  155.1 3.0 collective-permute-start.7
  169.0 7.7 %copy.46 = f32[256,27,256]{2,1,0:T(8,128)} copy(f32[256,27,256]{2,0,1:T(8,128)S(1)} %broadcast_multiply_fusion) | data formatting | bytes 14155776 | tf_op jit(solution)/shard_map/mul | solution.py:101
  176.7 8.5 %mul.17 = f32[6912,256]{1,0:T(8,128)} reshape(f32[256,27,256]{2,1,0:T(8,128)} %copy.46) | data formatting | bytes 14155776 | tf_op jit(solution)/shard_map/mul | solution.py:101
  185.2 293.6 %fusion.179 = (f32[56,256]{1,0:T(8,128)}, f32[56,256]{1,0:T(8,128)}) fusion(f32[6912,256]{1,0:T(8,128)} %mul.15, f32[6912,256]{1,0:T(8,128)} %mul.17), kind=kCustom, calls=%all-reduce-scatter.2 | all-reduce-scatter fusion | flops 3670017 | bytes 14270464
  480.2 4.4 collective-permute-start.21
  484.6 8.4 %collective-permute-start.22 = (f32[56,256]{1,0:T(8,128)}, f32[56,256]{1,0:T(8,128)}, u32[]{:S(2)}, u32[]{:S(2)}) collective-permute-start(f32[56,256]{1,0:T(8,128)} %get-tuple-element.15), channel_id=1, source_target_pairs={{0,2},{1,3},{2,4},{3,5},{4,6},{5,7},{6,8},{7,9},{8,10},{9,11},{10,... | collective-permute-start | bytes 172040
  493.0 10.4 %collective-permute-start.23 = (f32[56,256]{1,0:T(8,128)}, f32[56,256]{1,0:T(8,128)}, u32[]{:S(2)}, u32[]{:S(2)}) collective-permute-start(f32[56,256]{1,0:T(8,128)} %get-tuple-element.15), channel_id=1, source_target_pairs={{0,3},{1,4},{2,5},{3,6},{4,7},{5,8},{6,9},{7,10},{8,11},{9,12},{10... | collective-permute-start | bytes 172040
  503.4 11.3 %collective-permute-start.24 = (f32[56,256]{1,0:T(8,128)}, f32[56,256]{1,0:T(8,128)}, u32[]{:S(2)}, u32[]{:S(2)}) collective-permute-start(f32[56,256]{1,0:T(8,128)} %get-tuple-element.15), channel_id=1, source_target_pairs={{0,4},{1,5},{2,6},{3,7},{4,8},{5,9},{6,10},{7,11},{8,12},{9,13},{1... | collective-permute-start | bytes 172040
  514.7 16.8 %collective-permute-start.25 = (f32[30,256]{1,0:T(8,128)}, f32[30,256]{1,0:T(8,128)}, u32[]{:S(2)}, u32[]{:S(2)}) collective-permute-start(f32[30,256]{1,0:T(8,128)} %slice.943), channel_id=1, source_target_pairs={{0,5},{1,6},{2,7},{3,8},{4,9},{5,10},{6,11},{7,12},{8,13},{9,14},{... | collective-permute-start | bytes 92168
  531.9 2.5 fusion.180
  587.4 3.5 collective-permute-start.16
  590.9 8.7 %collective-permute-start.17 = (f32[56,256]{1,0:T(8,128)S(1)}, f32[56,256]{1,0:T(8,128)S(1)}, u32[]{:S(2)}, u32[]{:S(2)}) collective-permute-start(f32[56,256]{1,0:T(8,128)S(1)} %copy-done.41), channel_id=1, source_target_pairs={{0,2},{1,3},{2,4},{3,5},{4,6},{5,7},{6,8},{7,9},{8,10},{9,11},{10,... | collective-permute-start | bytes 172040
  599.6 8.4 %collective-permute-start.18 = (f32[56,256]{1,0:T(8,128)S(1)}, f32[56,256]{1,0:T(8,128)S(1)}, u32[]{:S(2)}, u32[]{:S(2)}) collective-permute-start(f32[56,256]{1,0:T(8,128)S(1)} %copy-done.41), channel_id=1, source_target_pairs={{0,3},{1,4},{2,5},{3,6},{4,7},{5,8},{6,9},{7,10},{8,11},{9,12},{10... | collective-permute-start | bytes 172040
  608.0 14.2 %collective-permute-start.19 = (f32[56,256]{1,0:T(8,128)S(1)}, f32[56,256]{1,0:T(8,128)S(1)}, u32[]{:S(2)}, u32[]{:S(2)}) collective-permute-start(f32[56,256]{1,0:T(8,128)S(1)} %copy-done.41), channel_id=1, source_target_pairs={{0,4},{1,5},{2,6},{3,7},{4,8},{5,9},{6,10},{7,11},{8,12},{9,13},{1... | collective-permute-start | bytes 172040
  622.3 14.3 %collective-permute-start.20 = (f32[30,256]{1,0:T(8,128)S(1)}, f32[30,256]{1,0:T(8,128)S(1)}, u32[]{:S(2)}, u32[]{:S(2)}) collective-permute-start(f32[30,256]{1,0:T(8,128)S(1)} %slice.942), channel_id=1, source_target_pairs={{0,5},{1,6},{2,7},{3,8},{4,9},{5,10},{6,11},{7,12},{8,13},{9,14},{... | collective-permute-start | bytes 92168
  636.5 5.1 concatenate.113
  641.7 31.1 %all-gather.1 = f32[16,54,256]{2,1,0:T(8,128)S(1)} all-gather(f32[1,54,256]{2,1,0:T(8,128)S(1)} %dynamic-slice_bitcast_fusion), channel_id=1, replica_groups=mesh['dp'=8,'ty'=4,'tz'=4] {'ty','tz'}, dimensions={0}, use_global_device_ids=true | all-gather | bytes 940032 | tf_op jit(solution)/shard_map/all_gather | solution.py:72
  675.2 35.9 %all-gather = f32[16,54,256]{2,1,0:T(8,128)S(1)} all-gather(f32[1,54,256]{2,1,0:T(8,128)S(1)} %dynamic-slice_bitcast_fusion.1), channel_id=1, replica_groups=mesh['dp'=8,'ty'=4,'tz'=4] {'ty','tz'}, dimensions={0}, use_global_device_ids=true | all-gather | bytes 940032 | tf_op jit(solution)/shard_map/all_gather | solution.py:72
  (344 shorter events, 156.6 us)
Async XLA Ops:
  7.2 68.9 %all-gather.5.cloned.1.call-start = ((), (), s32[]{:S(2)}) async-start(), calls=%async_computation | async-start | bytes 3981312 | tf_op jit(solution)/shard_map/all_gather | solution.py:92
  7.9 562.6 %all-gather.7.cloned.1.call-start = ((), (), s32[]{:S(2)}) async-start(), calls=%async_computation.1 | async-start | bytes 3981312 | tf_op jit(solution)/shard_map/all_gather | solution.py:103
  9.1 11.4 %collective-permute-start = (bf16[1,4,1,12,256]{4,3,2,1,0:T(8,128)(2,1)S(1)}, bf16[1,4,1,12,256]{4,3,2,1,0:T(8,128)(2,1)S(1)}, u32[]{:S(2)}, u32[]{:S(2)}) collective-permute-start(bf16[1,4,1,12,256]{4,3,2,1,0:T(8,128)(2,1)S(1)} %get-tuple-element.88), channel_id=1, source_target_pairs={{0,4},{4,8},{8,12},{1,5},{5,9},{9,13},{2,6},{6,10},{10,14},{3,7},{... | collective-permute-start | bytes 73736 | tf_op jit(solution)/shard_map/ppermute | solution.py:13
  10.9 9.6 %collective-permute-start.1 = (bf16[1,4,1,12,256]{4,3,2,1,0:T(8,128)(2,1)S(1)}, bf16[1,4,1,12,256]{4,3,2,1,0:T(8,128)(2,1)S(1)}, u32[]{:S(2)}, u32[]{:S(2)}) collective-permute-start(bf16[1,4,1,12,256]{4,3,2,1,0:T(8,128)(2,1)S(1)} %get-tuple-element.89), channel_id=1, source_target_pairs={{4,0},{8,4},{12,8},{5,1},{9,5},{13,9},{6,2},{10,6},{14,10},{7,3},{... | collective-permute-start | bytes 73736 | tf_op jit(solution)/shard_map/ppermute | solution.py:16
  13.9 12.5 %collective-permute-start.8 = (bf16[1,4,1,12,256]{4,3,2,1,0:T(8,128)(2,1)S(1)}, bf16[1,4,1,12,256]{4,3,2,1,0:T(8,128)(2,1)S(1)}, u32[]{:S(2)}, u32[]{:S(2)}) collective-permute-start(bf16[1,4,1,12,256]{4,3,2,1,0:T(8,128)(2,1)S(1)} %get-tuple-element.81), channel_id=1, source_target_pairs={{0,4},{4,8},{8,12},{1,5},{5,9},{9,13},{2,6},{6,10},{10,14},{3,7},{... | collective-permute-start | bytes 73736 | tf_op jit(solution)/shard_map/ppermute | solution.py:13
  18.4 9.2 %collective-permute-start.9 = (bf16[1,4,1,12,256]{4,3,2,1,0:T(8,128)(2,1)S(1)}, bf16[1,4,1,12,256]{4,3,2,1,0:T(8,128)(2,1)S(1)}, u32[]{:S(2)}, u32[]{:S(2)}) collective-permute-start(bf16[1,4,1,12,256]{4,3,2,1,0:T(8,128)(2,1)S(1)} %get-tuple-element.80), channel_id=1, source_target_pairs={{4,0},{8,4},{12,8},{5,1},{9,5},{13,9},{6,2},{10,6},{14,10},{7,3},{... | collective-permute-start | bytes 73736 | tf_op jit(solution)/shard_map/ppermute | solution.py:16
  20.5 17.3 %copy-start.37 = (bf16[1,4,1,12,256]{4,3,2,1,0:T(8,128)(2,1)}, bf16[1,4,1,12,256]{4,3,2,1,0:T(8,128)(2,1)S(1)}, u32[]{:S(2)}) copy-start(bf16[1,4,1,12,256]{4,3,2,1,0:T(8,128)(2,1)S(1)} %collective-permute-done) | copy-start | bytes 73732
  20.5 17.3 %copy-start.39 = (bf16[1,4,1,12,256]{4,3,2,1,0:T(8,128)(2,1)}, bf16[1,4,1,12,256]{4,3,2,1,0:T(8,128)(2,1)S(1)}, u32[]{:S(2)}) copy-start(bf16[1,4,1,12,256]{4,3,2,1,0:T(8,128)(2,1)S(1)} %collective-permute-done.1) | copy-start | bytes 73732
  20.6 17.1 %collective-permute-start.2 = (bf16[1,4,14,1,256]{4,3,2,1,0:T(2,128)(2,1)S(1)}, bf16[1,4,14,1,256]{4,3,2,1,0:T(2,128)(2,1)S(1)}, u32[]{:S(2)}, u32[]{:S(2)}) collective-permute-start(bf16[1,4,14,1,256]{4,3,2,1,0:T(2,128)(2,1)S(1)} %get-tuple-element.77), channel_id=1, source_target_pairs={{0,1},{1,2},{2,3},{4,5},{5,6},{6,7},{8,9},{9,10},{10,11},{12,13},{... | collective-permute-start | bytes 86024 | tf_op jit(solution)/shard_map/ppermute | solution.py:13
  24.0 13.7 %collective-permute-start.3 = (bf16[1,4,14,1,256]{4,3,2,1,0:T(2,128)(2,1)S(1)}, bf16[1,4,14,1,256]{4,3,2,1,0:T(2,128)(2,1)S(1)}, u32[]{:S(2)}, u32[]{:S(2)}) collective-permute-start(bf16[1,4,14,1,256]{4,3,2,1,0:T(2,128)(2,1)S(1)} %get-tuple-element.76), channel_id=1, source_target_pairs={{1,0},{2,1},{3,2},{5,4},{6,5},{7,6},{9,8},{10,9},{11,10},{13,12},{... | collective-permute-start | bytes 86024 | tf_op jit(solution)/shard_map/ppermute | solution.py:16
  31.3 42.5 %collective-permute-start.10 = (bf16[1,4,14,1,256]{4,3,2,1,0:T(2,128)(2,1)}, bf16[1,4,14,1,256]{4,3,2,1,0:T(2,128)(2,1)}, u32[]{:S(2)}, u32[]{:S(2)}) collective-permute-start(bf16[1,4,14,1,256]{4,3,2,1,0:T(2,128)(2,1)} %get-tuple-element.56), channel_id=1, source_target_pairs={{0,1},{1,2},{2,3},{4,5},{5,6},{6,7},{8,9},{9,10},{10,11},{12,13},{... | collective-permute-start | bytes 86024 | tf_op jit(solution)/shard_map/ppermute | solution.py:13
  34.7 39.1 %collective-permute-start.11 = (bf16[1,4,14,1,256]{4,3,2,1,0:T(2,128)(2,1)}, bf16[1,4,14,1,256]{4,3,2,1,0:T(2,128)(2,1)}, u32[]{:S(2)}, u32[]{:S(2)}) collective-permute-start(bf16[1,4,14,1,256]{4,3,2,1,0:T(2,128)(2,1)} %get-tuple-element.57), channel_id=1, source_target_pairs={{1,0},{2,1},{3,2},{5,4},{6,5},{7,6},{9,8},{10,9},{11,10},{13,12},{... | collective-permute-start | bytes 86024 | tf_op jit(solution)/shard_map/ppermute | solution.py:16
  94.2 50.5 %collective-permute-start.12 = (bf16[1,4,1,12,256]{4,3,2,1,0:T(8,128)(2,1)S(1)}, bf16[1,4,1,12,256]{4,3,2,1,0:T(8,128)(2,1)S(1)}, u32[]{:S(2)}, u32[]{:S(2)}) collective-permute-start(bf16[1,4,1,12,256]{4,3,2,1,0:T(8,128)(2,1)S(1)} %get-tuple-element.78), channel_id=1, source_target_pairs={{0,4},{4,8},{8,12},{1,5},{5,9},{9,13},{2,6},{6,10},{10,14},{3,7},{... | collective-permute-start | bytes 73736 | tf_op jit(solution)/shard_map/ppermute | solution.py:13
  97.4 47.2 %collective-permute-start.13 = (bf16[1,4,1,12,256]{4,3,2,1,0:T(8,128)(2,1)S(1)}, bf16[1,4,1,12,256]{4,3,2,1,0:T(8,128)(2,1)S(1)}, u32[]{:S(2)}, u32[]{:S(2)}) collective-permute-start(bf16[1,4,1,12,256]{4,3,2,1,0:T(8,128)(2,1)S(1)} %get-tuple-element.79), channel_id=1, source_target_pairs={{4,0},{8,4},{12,8},{5,1},{9,5},{13,9},{6,2},{10,6},{14,10},{7,3},{... | collective-permute-start | bytes 73736 | tf_op jit(solution)/shard_map/ppermute | solution.py:16
  138.1 12.5 %collective-permute-start.4 = (bf16[1,4,1,12,256]{4,3,2,1,0:T(8,128)(2,1)S(1)}, bf16[1,4,1,12,256]{4,3,2,1,0:T(8,128)(2,1)S(1)}, u32[]{:S(2)}, u32[]{:S(2)}) collective-permute-start(bf16[1,4,1,12,256]{4,3,2,1,0:T(8,128)(2,1)S(1)} %get-tuple-element.84), channel_id=1, source_target_pairs={{0,4},{4,8},{8,12},{1,5},{5,9},{9,13},{2,6},{6,10},{10,14},{3,7},{... | collective-permute-start | bytes 73736 | tf_op jit(solution)/shard_map/ppermute | solution.py:13
  143.3 7.3 %collective-permute-start.5 = (bf16[1,4,1,12,256]{4,3,2,1,0:T(8,128)(2,1)S(1)}, bf16[1,4,1,12,256]{4,3,2,1,0:T(8,128)(2,1)S(1)}, u32[]{:S(2)}, u32[]{:S(2)}) collective-permute-start(bf16[1,4,1,12,256]{4,3,2,1,0:T(8,128)(2,1)S(1)} %get-tuple-element.85), channel_id=1, source_target_pairs={{4,0},{8,4},{12,8},{5,1},{9,5},{13,9},{6,2},{10,6},{14,10},{7,3},{... | collective-permute-start | bytes 73736 | tf_op jit(solution)/shard_map/ppermute | solution.py:16
  144.8 13.4 %collective-permute-start.14 = (bf16[1,4,14,1,256]{4,3,2,1,0:T(2,128)(2,1)S(1)}, bf16[1,4,14,1,256]{4,3,2,1,0:T(2,128)(2,1)S(1)}, u32[]{:S(2)}, u32[]{:S(2)}) collective-permute-start(bf16[1,4,14,1,256]{4,3,2,1,0:T(2,128)(2,1)S(1)} %get-tuple-element.54), channel_id=1, source_target_pairs={{0,1},{1,2},{2,3},{4,5},{5,6},{6,7},{8,9},{9,10},{10,11},{12,13},{... | collective-permute-start | bytes 86024 | tf_op jit(solution)/shard_map/ppermute | solution.py:13
  147.7 10.5 %collective-permute-start.15 = (bf16[1,4,14,1,256]{4,3,2,1,0:T(2,128)(2,1)S(1)}, bf16[1,4,14,1,256]{4,3,2,1,0:T(2,128)(2,1)S(1)}, u32[]{:S(2)}, u32[]{:S(2)}) collective-permute-start(bf16[1,4,14,1,256]{4,3,2,1,0:T(2,128)(2,1)S(1)} %get-tuple-element.55), channel_id=1, source_target_pairs={{1,0},{2,1},{3,2},{5,4},{6,5},{7,6},{9,8},{10,9},{11,10},{13,12},{... | collective-permute-start | bytes 86024 | tf_op jit(solution)/shard_map/ppermute | solution.py:16
  150.6 380.8 %copy-start.36 = (bf16[1,4,1,12,256]{4,3,2,1,0:T(8,128)(2,1)}, bf16[1,4,1,12,256]{4,3,2,1,0:T(8,128)(2,1)S(1)}, u32[]{:S(2)}) copy-start(bf16[1,4,1,12,256]{4,3,2,1,0:T(8,128)(2,1)S(1)} %collective-permute-done.5) | copy-start | bytes 73732
  152.3 351.1 %collective-permute-start.6 = (bf16[1,4,14,1,256]{4,3,2,1,0:T(2,128)(2,1)}, bf16[1,4,14,1,256]{4,3,2,1,0:T(2,128)(2,1)S(1)}, u32[]{:S(2)}, u32[]{:S(2)}) collective-permute-start(bf16[1,4,14,1,256]{4,3,2,1,0:T(2,128)(2,1)} %get-tuple-element.67), channel_id=1, source_target_pairs={{0,1},{1,2},{2,3},{4,5},{5,6},{6,7},{8,9},{9,10},{10,11},{12,13},{... | collective-permute-start | bytes 86024 | tf_op jit(solution)/shard_map/ppermute | solution.py:13
  155.1 359.5 %collective-permute-start.7 = (bf16[1,4,14,1,256]{4,3,2,1,0:T(2,128)(2,1)}, bf16[1,4,14,1,256]{4,3,2,1,0:T(2,128)(2,1)S(1)}, u32[]{:S(2)}, u32[]{:S(2)}) collective-permute-start(bf16[1,4,14,1,256]{4,3,2,1,0:T(2,128)(2,1)} %get-tuple-element.66), channel_id=1, source_target_pairs={{1,0},{2,1},{3,2},{5,4},{6,5},{7,6},{9,8},{10,9},{11,10},{13,12},{... | collective-permute-start | bytes 86024 | tf_op jit(solution)/shard_map/ppermute | solution.py:16
  480.2 110.7 %collective-permute-start.21 = (f32[56,256]{1,0:T(8,128)}, f32[56,256]{1,0:T(8,128)}, u32[]{:S(2)}, u32[]{:S(2)}) collective-permute-start(f32[56,256]{1,0:T(8,128)} %get-tuple-element.15), channel_id=1, source_target_pairs={{0,1},{1,2},{2,3},{3,4},{4,5},{5,6},{6,7},{7,8},{8,9},{9,10},{10,1... | collective-permute-start | bytes 172040
  484.6 115.1 %collective-permute-start.22 = (f32[56,256]{1,0:T(8,128)}, f32[56,256]{1,0:T(8,128)}, u32[]{:S(2)}, u32[]{:S(2)}) collective-permute-start(f32[56,256]{1,0:T(8,128)} %get-tuple-element.15), channel_id=1, source_target_pairs={{0,2},{1,3},{2,4},{3,5},{4,6},{5,7},{6,8},{7,9},{8,10},{9,11},{10,... | collective-permute-start | bytes 172040
  493.0 115.1 %collective-permute-start.23 = (f32[56,256]{1,0:T(8,128)}, f32[56,256]{1,0:T(8,128)}, u32[]{:S(2)}, u32[]{:S(2)}) collective-permute-start(f32[56,256]{1,0:T(8,128)} %get-tuple-element.15), channel_id=1, source_target_pairs={{0,3},{1,4},{2,5},{3,6},{4,7},{5,8},{6,9},{7,10},{8,11},{9,12},{10... | collective-permute-start | bytes 172040
  503.4 28.1 %copy-start.43 = (bf16[1,4,14,1,256]{4,3,2,1,0:T(2,128)(2,1)}, bf16[1,4,14,1,256]{4,3,2,1,0:T(2,128)(2,1)S(1)}, u32[]{:S(2)}) copy-start(bf16[1,4,14,1,256]{4,3,2,1,0:T(2,128)(2,1)S(1)} %collective-permute-done.6) | copy-start | bytes 86020
  503.4 118.9 %collective-permute-start.24 = (f32[56,256]{1,0:T(8,128)}, f32[56,256]{1,0:T(8,128)}, u32[]{:S(2)}, u32[]{:S(2)}) collective-permute-start(f32[56,256]{1,0:T(8,128)} %get-tuple-element.15), channel_id=1, source_target_pairs={{0,4},{1,5},{2,6},{3,7},{4,8},{5,9},{6,10},{7,11},{8,12},{9,13},{1... | collective-permute-start | bytes 172040
  514.7 72.7 %collective-permute-start.25 = (f32[30,256]{1,0:T(8,128)}, f32[30,256]{1,0:T(8,128)}, u32[]{:S(2)}, u32[]{:S(2)}) collective-permute-start(f32[30,256]{1,0:T(8,128)} %slice.943), channel_id=1, source_target_pairs={{0,5},{1,6},{2,7},{3,8},{4,9},{5,10},{6,11},{7,12},{8,13},{9,14},{... | collective-permute-start | bytes 92168
  587.4 86.9 %collective-permute-start.16 = (f32[56,256]{1,0:T(8,128)S(1)}, f32[56,256]{1,0:T(8,128)S(1)}, u32[]{:S(2)}, u32[]{:S(2)}) collective-permute-start(f32[56,256]{1,0:T(8,128)S(1)} %copy-done.41), channel_id=1, source_target_pairs={{0,1},{1,2},{2,3},{3,4},{4,5},{5,6},{6,7},{7,8},{8,9},{9,10},{10,1... | collective-permute-start | bytes 172040
  590.9 83.4 %collective-permute-start.17 = (f32[56,256]{1,0:T(8,128)S(1)}, f32[56,256]{1,0:T(8,128)S(1)}, u32[]{:S(2)}, u32[]{:S(2)}) collective-permute-start(f32[56,256]{1,0:T(8,128)S(1)} %copy-done.41), channel_id=1, source_target_pairs={{0,2},{1,3},{2,4},{3,5},{4,6},{5,7},{6,8},{7,9},{8,10},{9,11},{10,... | collective-permute-start | bytes 172040
  599.6 74.7 %collective-permute-start.18 = (f32[56,256]{1,0:T(8,128)S(1)}, f32[56,256]{1,0:T(8,128)S(1)}, u32[]{:S(2)}, u32[]{:S(2)}) collective-permute-start(f32[56,256]{1,0:T(8,128)S(1)} %copy-done.41), channel_id=1, source_target_pairs={{0,3},{1,4},{2,5},{3,6},{4,7},{5,8},{6,9},{7,10},{8,11},{9,12},{10... | collective-permute-start | bytes 172040
  608.0 66.3 %collective-permute-start.19 = (f32[56,256]{1,0:T(8,128)S(1)}, f32[56,256]{1,0:T(8,128)S(1)}, u32[]{:S(2)}, u32[]{:S(2)}) collective-permute-start(f32[56,256]{1,0:T(8,128)S(1)} %copy-done.41), channel_id=1, source_target_pairs={{0,4},{1,5},{2,6},{3,7},{4,8},{5,9},{6,10},{7,11},{8,12},{9,13},{1... | collective-permute-start | bytes 172040
  622.3 52.0 %collective-permute-start.20 = (f32[30,256]{1,0:T(8,128)S(1)}, f32[30,256]{1,0:T(8,128)S(1)}, u32[]{:S(2)}, u32[]{:S(2)}) collective-permute-start(f32[30,256]{1,0:T(8,128)S(1)} %slice.942), channel_id=1, source_target_pairs={{0,5},{1,6},{2,7},{3,8},{4,9},{5,10},{6,11},{7,12},{8,13},{9,14},{... | collective-permute-start | bytes 92168
  (49 other events, 241.3 us)
Sparse Core Ops, SparseCore 0:
  10.3 63.1 all-gather.4
  75.9 64.0 all-gather.6
where the time goes:
time: 731 us; the launch traced here: 720 us
  blocking collectives  361 us (49%)
  starting transfers between devices  145 us (20%)
  local copies, waits for them, and re-layouts  129 us (18%)
  matrix products  55.2 us (8%)
  between operations  16.4 us (2%)
  other arithmetic  13.1 us (2%)
    unnamed x1, blocking collectives  294 us
    unnamed x10, starting transfers between devices  100 us
    all_gather x2, blocking collectives, reduce_terms(): whole = lax.all_gather(share, ('ty', 'tz'), axis=0, tiled=True)  66.9 us
    reshape x54, local copies, waits for them, and re-layouts, transpose_maker(): sliced = window(grad_pad, back, shape).reshape(-1, grad_pad.shape[4])  66.5 us
    dot_general x54, matrix products, transpose_maker(): lax.dot_general(sliced, piece[:, index, :], (((1,), (1,)), ((), ())), pre...  31.8 us
    ppermute x8, starting transfers between devices, extended(): lax.ppermute(lax.slice_in_dim(block, block.shape[dim] - width, None, axis...  27.1 us
    dot_general x54, matrix products, filter_from_inputs(): lax.dot_general(sliced, flat_grad, (((0,), (0,)), ((), ())), preferred_el...  23.5 us
    mul x2, local copies, waits for them, and re-layouts, local(): grad_w_first = reduce_terms(part_first * scale)  19.2 us
  transfers between devices with their start and end apart: 28, of which 0 were waited for; matrix products, arithmetic and copies ran while one was open for 67% of the time, Pallas kernels for 0%

commit v1 on v0

--- a/solution.py
+++ b/solution.py
@@ -69,7 +69,10 @@
     ch_in, tap_count, ch_out = partial_value.shape
     flat = partial_value.reshape(ch_in * tap_count, ch_out)
     share = lax.psum_scatter(flat, ("dp", "ty", "tz"), scatter_dimension=0, tiled=True)
-    whole = lax.all_gather(share, ("ty", "tz"), axis=0, tiled=True)
+    n_dev = lax.axis_size(("ty", "tz"))
+    shards = jnp.stack([share for _ in range(n_dev)])
+    shards = lax.all_to_all(shards, ("ty", "tz"), split_axis=0, concat_axis=0)
+    whole = jnp.concatenate(shards, axis=0)
     return whole.reshape(-1, tap_count, ch_out)
 
 

time: 731 us -> 689 us (0.943)
  blocking collectives: 361 us -> 294 us
  waiting for transfers between devices: 0.79 us -> 12.1 us
  starting transfers between devices: 145 us -> 154 us
    all_gather x2 -> x0, blocking collectives: 66.9 us -> none  [reduce_terms(): whole = lax.all_gather(share, ('ty', 'tz'), axis=0, tiled=True)]
    all_to_all x0 -> x2, waiting for transfers between devices: none -> 11.3 us  [reduce_terms(): shards = lax.all_to_all(shards, ('ty', 'tz'), split_axis=0, concat_axis=0)]
    all_to_all x0 -> x2, starting transfers between devices: none -> 9.14 us  [reduce_terms(): shards = lax.all_to_all(shards, ('ty', 'tz'), split_axis=0, concat_axis=0)]
  transfers between devices with their start and end apart: 28 -> 30, of which waited for: 0 -> 2; matrix products, arithmetic and copies ran while one was open for 67% -> 72% of each run, Pallas kernels for 0% -> 0%
where the time goes in v1:
time: 689 us; the launch traced here: 677 us
  blocking collectives  294 us (43%)
  starting transfers between devices  154 us (22%)
  local copies, waits for them, and re-layouts  129 us (19%)
  matrix products  59.8 us (9%)
  between operations  16.5 us (2%)
  other arithmetic  12.4 us (2%)
  waiting for transfers between devices  12.1 us (2%)
    unnamed x1, blocking collectives  294 us
    unnamed x10, starting transfers between devices  100 us
    reshape x54, local copies, waits for them, and re-layouts, transpose_maker(): sliced = window(grad_pad, back, shape).reshape(-1, grad_pad.shape[4])  64.1 us
    dot_general x54, matrix products, transpose_maker(): lax.dot_general(sliced, piece[:, index, :], (((1,), (1,)), ((), ())), pre...  36.4 us
    ppermute x8, starting transfers between devices, extended(): lax.ppermute(lax.slice_in_dim(block, block.shape[dim] - width, None, axis...  27.1 us
    dot_general x54, matrix products, filter_from_inputs(): lax.dot_general(sliced, flat_grad, (((0,), (0,)), ((), ())), preferred_el...  23.5 us
    mul x2, local copies, waits for them, and re-layouts, local(): grad_w_first = reduce_terms(part_first * scale)  19.2 us
    unnamed x118, local copies, waits for them, and re-layouts  17.9 us
  transfers between devices with their start and end apart: 30, of which 2 were waited for; matrix products, arithmetic and copies ran while one was open for 72% of the time, Pallas kernels for 0%

profile of v1, /device:TPU:82, one launch (start us, length us, event | category | flops | bytes accessed | tf_op | source)
XLA Modules:
  0.0 677.2 jit_solution(12183429948409983282)
XLA Ops:
  14.0 4.4 collective-permute-start.8
  20.6 3.4 collective-permute-start.2
  31.3 3.4 collective-permute-start.10
  34.7 3.1 collective-permute-start.11
  94.1 3.2 collective-permute-start.12
  114.7 3.4 broadcast_multiply_fusion.1
  118.9 10.7 %copy.44 = f32[256,27,256]{2,1,0:T(8,128)} copy(f32[256,27,256]{2,0,1:T(8,128)} %broadcast_multiply_fusion.1) | data formatting | bytes 14155776 | tf_op jit(solution)/shard_map/mul | solution.py:108
  129.6 8.5 %mul.15 = f32[6912,256]{1,0:T(8,128)} reshape(f32[256,27,256]{2,1,0:T(8,128)} %copy.44) | data formatting | bytes 14155776 | tf_op jit(solution)/shard_map/mul | solution.py:108
  138.1 5.3 collective-permute-start.4
  144.8 2.8 collective-permute-start.14
  147.6 3.0 collective-permute-start.15
  151.7 2.8 collective-permute-start.6
  154.5 3.0 collective-permute-start.7
  168.4 7.7 %copy.46 = f32[256,27,256]{2,1,0:T(8,128)} copy(f32[256,27,256]{2,0,1:T(8,128)S(1)} %broadcast_multiply_fusion) | data formatting | bytes 14155776 | tf_op jit(solution)/shard_map/mul | solution.py:104
  176.1 8.5 %mul.17 = f32[6912,256]{1,0:T(8,128)} reshape(f32[256,27,256]{2,1,0:T(8,128)} %copy.46) | data formatting | bytes 14155776 | tf_op jit(solution)/shard_map/mul | solution.py:104
  184.6 293.5 %fusion.179 = (f32[56,256]{1,0:T(8,128)}, f32[56,256]{1,0:T(8,128)}) fusion(f32[6912,256]{1,0:T(8,128)} %mul.15, f32[6912,256]{1,0:T(8,128)} %mul.17), kind=kCustom, calls=%all-reduce-scatter.2 | all-reduce-scatter fusion | flops 3670017 | bytes 14270464
  479.5 4.4 collective-permute-start.21
  483.9 8.0 %collective-permute-start.22 = (f32[56,256]{1,0:T(8,128)}, f32[56,256]{1,0:T(8,128)}, u32[]{:S(2)}, u32[]{:S(2)}) collective-permute-start(f32[56,256]{1,0:T(8,128)} %get-tuple-element.15), channel_id=1, source_target_pairs={{0,2},{1,3},{2,4},{3,5},{4,6},{5,7},{6,8},{7,9},{8,10},{9,11},{10,... | collective-permute-start | bytes 172040
  491.9 10.9 %collective-permute-start.23 = (f32[56,256]{1,0:T(8,128)}, f32[56,256]{1,0:T(8,128)}, u32[]{:S(2)}, u32[]{:S(2)}) collective-permute-start(f32[56,256]{1,0:T(8,128)} %get-tuple-element.15), channel_id=1, source_target_pairs={{0,3},{1,4},{2,5},{3,6},{4,7},{5,8},{6,9},{7,10},{8,11},{9,12},{10... | collective-permute-start | bytes 172040
  502.9 11.3 %collective-permute-start.24 = (f32[56,256]{1,0:T(8,128)}, f32[56,256]{1,0:T(8,128)}, u32[]{:S(2)}, u32[]{:S(2)}) collective-permute-start(f32[56,256]{1,0:T(8,128)} %get-tuple-element.15), channel_id=1, source_target_pairs={{0,4},{1,5},{2,6},{3,7},{4,8},{5,9},{6,10},{7,11},{8,12},{9,13},{1... | collective-permute-start | bytes 172040
  514.2 17.1 %collective-permute-start.25 = (f32[30,256]{1,0:T(8,128)}, f32[30,256]{1,0:T(8,128)}, u32[]{:S(2)}, u32[]{:S(2)}) collective-permute-start(f32[30,256]{1,0:T(8,128)} %slice.943), channel_id=1, source_target_pairs={{0,5},{1,6},{2,7},{3,8},{4,9},{5,10},{6,11},{7,12},{8,13},{9,14},{... | collective-permute-start | bytes 92168
  531.7 2.5 fusion.180
  576.8 3.1 collective-permute-start.16
  579.9 8.7 %collective-permute-start.17 = (f32[56,256]{1,0:T(8,128)S(1)}, f32[56,256]{1,0:T(8,128)S(1)}, u32[]{:S(2)}, u32[]{:S(2)}) collective-permute-start(f32[56,256]{1,0:T(8,128)S(1)} %copy-done.41), channel_id=1, source_target_pairs={{0,2},{1,3},{2,4},{3,5},{4,6},{5,7},{6,8},{7,9},{8,10},{9,11},{10,... | collective-permute-start | bytes 172040
  588.7 8.2 %collective-permute-start.18 = (f32[56,256]{1,0:T(8,128)S(1)}, f32[56,256]{1,0:T(8,128)S(1)}, u32[]{:S(2)}, u32[]{:S(2)}) collective-permute-start(f32[56,256]{1,0:T(8,128)S(1)} %copy-done.41), channel_id=1, source_target_pairs={{0,3},{1,4},{2,5},{3,6},{4,7},{5,8},{6,9},{7,10},{8,11},{9,12},{10... | collective-permute-start | bytes 172040
  596.9 14.2 %collective-permute-start.19 = (f32[56,256]{1,0:T(8,128)S(1)}, f32[56,256]{1,0:T(8,128)S(1)}, u32[]{:S(2)}, u32[]{:S(2)}) collective-permute-start(f32[56,256]{1,0:T(8,128)S(1)} %copy-done.41), channel_id=1, source_target_pairs={{0,4},{1,5},{2,6},{3,7},{4,8},{5,9},{6,10},{7,11},{8,12},{9,13},{1... | collective-permute-start | bytes 172040
  611.1 14.3 %collective-permute-start.20 = (f32[30,256]{1,0:T(8,128)}, f32[30,256]{1,0:T(8,128)S(1)}, u32[]{:S(2)}, u32[]{:S(2)}) collective-permute-start(f32[30,256]{1,0:T(8,128)} %slice.942), channel_id=1, source_target_pairs={{0,5},{1,6},{2,7},{3,8},{4,9},{5,10},{6,11},{7,12},{8,13},{9,14},{... | collective-permute-start | bytes 92168
  625.5 5.1 concatenate.113
  631.6 3.9 all-to-all-start.1
  640.7 8.3 %all-to-all-done.1 = f32[16,54,256]{2,1,0:T(8,128)S(1)} async-done(((f32[16,54,256]{2,1,0:T(8,128)}), f32[16,54,256]{2,1,0:T(8,128)S(1)}, u32[]{:S(2)}, u32[]{:S(2)}) %all-to-all-start.1) | async-done | bytes 884768 | tf_op jit(solution)/shard_map/all_to_all | solution.py:74
  649.9 5.2 all-to-all-start
  665.5 3.1 all-to-all-done
  (348 shorter events, 165.6 us)
Async XLA Ops:
  7.2 68.9 %all-gather.3.cloned.1.call-start = ((), (), s32[]{:S(2)}) async-start(), calls=%async_computation.2 | async-start | bytes 3981312 | tf_op jit(solution)/shard_map/all_gather | solution.py:95
  7.9 556.0 %all-gather.5.cloned.1.call-start = ((), (), s32[]{:S(2)}) async-start(), calls=%async_computation.3 | async-start | bytes 3981312 | tf_op jit(solution)/shard_map/all_gather | solution.py:106
  9.1 11.4 %collective-permute-start = (bf16[1,4,1,12,256]{4,3,2,1,0:T(8,128)(2,1)S(1)}, bf16[1,4,1,12,256]{4,3,2,1,0:T(8,128)(2,1)S(1)}, u32[]{:S(2)}, u32[]{:S(2)}) collective-permute-start(bf16[1,4,1,12,256]{4,3,2,1,0:T(8,128)(2,1)S(1)} %get-tuple-element.88), channel_id=1, source_target_pairs={{0,4},{4,8},{8,12},{1,5},{5,9},{9,13},{2,6},{6,10},{10,14},{3,7},{... | collective-permute-start | bytes 73736 | tf_op jit(solution)/shard_map/ppermute | solution.py:13
  10.9 9.6 %collective-permute-start.1 = (bf16[1,4,1,12,256]{4,3,2,1,0:T(8,128)(2,1)S(1)}, bf16[1,4,1,12,256]{4,3,2,1,0:T(8,128)(2,1)S(1)}, u32[]{:S(2)}, u32[]{:S(2)}) collective-permute-start(bf16[1,4,1,12,256]{4,3,2,1,0:T(8,128)(2,1)S(1)} %get-tuple-element.89), channel_id=1, source_target_pairs={{4,0},{8,4},{12,8},{5,1},{9,5},{13,9},{6,2},{10,6},{14,10},{7,3},{... | collective-permute-start | bytes 73736 | tf_op jit(solution)/shard_map/ppermute | solution.py:16
  14.0 12.5 %collective-permute-start.8 = (bf16[1,4,1,12,256]{4,3,2,1,0:T(8,128)(2,1)S(1)}, bf16[1,4,1,12,256]{4,3,2,1,0:T(8,128)(2,1)S(1)}, u32[]{:S(2)}, u32[]{:S(2)}) collective-permute-start(bf16[1,4,1,12,256]{4,3,2,1,0:T(8,128)(2,1)S(1)} %get-tuple-element.81), channel_id=1, source_target_pairs={{0,4},{4,8},{8,12},{1,5},{5,9},{9,13},{2,6},{6,10},{10,14},{3,7},{... | collective-permute-start | bytes 73736 | tf_op jit(solution)/shard_map/ppermute | solution.py:13
  18.4 9.2 %collective-permute-start.9 = (bf16[1,4,1,12,256]{4,3,2,1,0:T(8,128)(2,1)S(1)}, bf16[1,4,1,12,256]{4,3,2,1,0:T(8,128)(2,1)S(1)}, u32[]{:S(2)}, u32[]{:S(2)}) collective-permute-start(bf16[1,4,1,12,256]{4,3,2,1,0:T(8,128)(2,1)S(1)} %get-tuple-element.80), channel_id=1, source_target_pairs={{4,0},{8,4},{12,8},{5,1},{9,5},{13,9},{6,2},{10,6},{14,10},{7,3},{... | collective-permute-start | bytes 73736 | tf_op jit(solution)/shard_map/ppermute | solution.py:16
  20.6 17.1 %collective-permute-start.2 = (bf16[1,4,14,1,256]{4,3,2,1,0:T(2,128)(2,1)S(1)}, bf16[1,4,14,1,256]{4,3,2,1,0:T(2,128)(2,1)S(1)}, u32[]{:S(2)}, u32[]{:S(2)}) collective-permute-start(bf16[1,4,14,1,256]{4,3,2,1,0:T(2,128)(2,1)S(1)} %get-tuple-element.77), channel_id=1, source_target_pairs={{0,1},{1,2},{2,3},{4,5},{5,6},{6,7},{8,9},{9,10},{10,11},{12,13},{... | collective-permute-start | bytes 86024 | tf_op jit(solution)/shard_map/ppermute | solution.py:13
  24.0 13.7 %collective-permute-start.3 = (bf16[1,4,14,1,256]{4,3,2,1,0:T(2,128)(2,1)S(1)}, bf16[1,4,14,1,256]{4,3,2,1,0:T(2,128)(2,1)S(1)}, u32[]{:S(2)}, u32[]{:S(2)}) collective-permute-start(bf16[1,4,14,1,256]{4,3,2,1,0:T(2,128)(2,1)S(1)} %get-tuple-element.76), channel_id=1, source_target_pairs={{1,0},{2,1},{3,2},{5,4},{6,5},{7,6},{9,8},{10,9},{11,10},{13,12},{... | collective-permute-start | bytes 86024 | tf_op jit(solution)/shard_map/ppermute | solution.py:16
  31.3 42.5 %collective-permute-start.10 = (bf16[1,4,14,1,256]{4,3,2,1,0:T(2,128)(2,1)}, bf16[1,4,14,1,256]{4,3,2,1,0:T(2,128)(2,1)}, u32[]{:S(2)}, u32[]{:S(2)}) collective-permute-start(bf16[1,4,14,1,256]{4,3,2,1,0:T(2,128)(2,1)} %get-tuple-element.56), channel_id=1, source_target_pairs={{0,1},{1,2},{2,3},{4,5},{5,6},{6,7},{8,9},{9,10},{10,11},{12,13},{... | collective-permute-start | bytes 86024 | tf_op jit(solution)/shard_map/ppermute | solution.py:13
  34.7 39.1 %collective-permute-start.11 = (bf16[1,4,14,1,256]{4,3,2,1,0:T(2,128)(2,1)}, bf16[1,4,14,1,256]{4,3,2,1,0:T(2,128)(2,1)}, u32[]{:S(2)}, u32[]{:S(2)}) collective-permute-start(bf16[1,4,14,1,256]{4,3,2,1,0:T(2,128)(2,1)} %get-tuple-element.57), channel_id=1, source_target_pairs={{1,0},{2,1},{3,2},{5,4},{6,5},{7,6},{9,8},{10,9},{11,10},{13,12},{... | collective-permute-start | bytes 86024 | tf_op jit(solution)/shard_map/ppermute | solution.py:16
  94.1 50.6 %collective-permute-start.12 = (bf16[1,4,1,12,256]{4,3,2,1,0:T(8,128)(2,1)S(1)}, bf16[1,4,1,12,256]{4,3,2,1,0:T(8,128)(2,1)S(1)}, u32[]{:S(2)}, u32[]{:S(2)}) collective-permute-start(bf16[1,4,1,12,256]{4,3,2,1,0:T(8,128)(2,1)S(1)} %get-tuple-element.78), channel_id=1, source_target_pairs={{0,4},{4,8},{8,12},{1,5},{5,9},{9,13},{2,6},{6,10},{10,14},{3,7},{... | collective-permute-start | bytes 73736 | tf_op jit(solution)/shard_map/ppermute | solution.py:13
  97.3 47.3 %collective-permute-start.13 = (bf16[1,4,1,12,256]{4,3,2,1,0:T(8,128)(2,1)S(1)}, bf16[1,4,1,12,256]{4,3,2,1,0:T(8,128)(2,1)S(1)}, u32[]{:S(2)}, u32[]{:S(2)}) collective-permute-start(bf16[1,4,1,12,256]{4,3,2,1,0:T(8,128)(2,1)S(1)} %get-tuple-element.79), channel_id=1, source_target_pairs={{4,0},{8,4},{12,8},{5,1},{9,5},{13,9},{6,2},{10,6},{14,10},{7,3},{... | collective-permute-start | bytes 73736 | tf_op jit(solution)/shard_map/ppermute | solution.py:16
  138.1 12.6 %collective-permute-start.4 = (bf16[1,4,1,12,256]{4,3,2,1,0:T(8,128)(2,1)S(1)}, bf16[1,4,1,12,256]{4,3,2,1,0:T(8,128)(2,1)S(1)}, u32[]{:S(2)}, u32[]{:S(2)}) collective-permute-start(bf16[1,4,1,12,256]{4,3,2,1,0:T(8,128)(2,1)S(1)} %get-tuple-element.84), channel_id=1, source_target_pairs={{0,4},{4,8},{8,12},{1,5},{5,9},{9,13},{2,6},{6,10},{10,14},{3,7},{... | collective-permute-start | bytes 73736 | tf_op jit(solution)/shard_map/ppermute | solution.py:13
  143.4 7.3 %collective-permute-start.5 = (bf16[1,4,1,12,256]{4,3,2,1,0:T(8,128)(2,1)S(1)}, bf16[1,4,1,12,256]{4,3,2,1,0:T(8,128)(2,1)S(1)}, u32[]{:S(2)}, u32[]{:S(2)}) collective-permute-start(bf16[1,4,1,12,256]{4,3,2,1,0:T(8,128)(2,1)S(1)} %get-tuple-element.85), channel_id=1, source_target_pairs={{4,0},{8,4},{12,8},{5,1},{9,5},{13,9},{6,2},{10,6},{14,10},{7,3},{... | collective-permute-start | bytes 73736 | tf_op jit(solution)/shard_map/ppermute | solution.py:16
  144.8 12.8 %collective-permute-start.14 = (bf16[1,4,14,1,256]{4,3,2,1,0:T(2,128)(2,1)S(1)}, bf16[1,4,14,1,256]{4,3,2,1,0:T(2,128)(2,1)S(1)}, u32[]{:S(2)}, u32[]{:S(2)}) collective-permute-start(bf16[1,4,14,1,256]{4,3,2,1,0:T(2,128)(2,1)S(1)} %get-tuple-element.54), channel_id=1, source_target_pairs={{0,1},{1,2},{2,3},{4,5},{5,6},{6,7},{8,9},{9,10},{10,11},{12,13},{... | collective-permute-start | bytes 86024 | tf_op jit(solution)/shard_map/ppermute | solution.py:13
  147.6 9.9 %collective-permute-start.15 = (bf16[1,4,14,1,256]{4,3,2,1,0:T(2,128)(2,1)S(1)}, bf16[1,4,14,1,256]{4,3,2,1,0:T(2,128)(2,1)S(1)}, u32[]{:S(2)}, u32[]{:S(2)}) collective-permute-start(bf16[1,4,14,1,256]{4,3,2,1,0:T(2,128)(2,1)S(1)} %get-tuple-element.55), channel_id=1, source_target_pairs={{1,0},{2,1},{3,2},{5,4},{6,5},{7,6},{9,8},{10,9},{11,10},{13,12},{... | collective-permute-start | bytes 86024 | tf_op jit(solution)/shard_map/ppermute | solution.py:16
  150.7 380.7 %copy-start.34 = (bf16[1,4,1,12,256]{4,3,2,1,0:T(8,128)(2,1)}, bf16[1,4,1,12,256]{4,3,2,1,0:T(8,128)(2,1)S(1)}, u32[]{:S(2)}) copy-start(bf16[1,4,1,12,256]{4,3,2,1,0:T(8,128)(2,1)S(1)} %collective-permute-done.4) | copy-start | bytes 73732
  150.7 380.7 %copy-start.36 = (bf16[1,4,1,12,256]{4,3,2,1,0:T(8,128)(2,1)}, bf16[1,4,1,12,256]{4,3,2,1,0:T(8,128)(2,1)S(1)}, u32[]{:S(2)}) copy-start(bf16[1,4,1,12,256]{4,3,2,1,0:T(8,128)(2,1)S(1)} %collective-permute-done.5) | copy-start | bytes 73732
  151.7 351.2 %collective-permute-start.6 = (bf16[1,4,14,1,256]{4,3,2,1,0:T(2,128)(2,1)S(1)}, bf16[1,4,14,1,256]{4,3,2,1,0:T(2,128)(2,1)S(1)}, u32[]{:S(2)}, u32[]{:S(2)}) collective-permute-start(bf16[1,4,14,1,256]{4,3,2,1,0:T(2,128)(2,1)S(1)} %get-tuple-element.67), channel_id=1, source_target_pairs={{0,1},{1,2},{2,3},{4,5},{5,6},{6,7},{8,9},{9,10},{10,11},{12,13},{... | collective-permute-start | bytes 86024 | tf_op jit(solution)/shard_map/ppermute | solution.py:13
  154.5 359.7 %collective-permute-start.7 = (bf16[1,4,14,1,256]{4,3,2,1,0:T(2,128)(2,1)S(1)}, bf16[1,4,14,1,256]{4,3,2,1,0:T(2,128)(2,1)S(1)}, u32[]{:S(2)}, u32[]{:S(2)}) collective-permute-start(bf16[1,4,14,1,256]{4,3,2,1,0:T(2,128)(2,1)S(1)} %get-tuple-element.66), channel_id=1, source_target_pairs={{1,0},{2,1},{3,2},{5,4},{6,5},{7,6},{9,8},{10,9},{11,10},{13,12},{... | collective-permute-start | bytes 86024 | tf_op jit(solution)/shard_map/ppermute | solution.py:16
  479.5 100.5 %collective-permute-start.21 = (f32[56,256]{1,0:T(8,128)}, f32[56,256]{1,0:T(8,128)}, u32[]{:S(2)}, u32[]{:S(2)}) collective-permute-start(f32[56,256]{1,0:T(8,128)} %get-tuple-element.15), channel_id=1, source_target_pairs={{0,1},{1,2},{2,3},{3,4},{4,5},{5,6},{6,7},{7,8},{8,9},{9,10},{10,1... | collective-permute-start | bytes 172040
  483.9 104.8 %collective-permute-start.22 = (f32[56,256]{1,0:T(8,128)}, f32[56,256]{1,0:T(8,128)}, u32[]{:S(2)}, u32[]{:S(2)}) collective-permute-start(f32[56,256]{1,0:T(8,128)} %get-tuple-element.15), channel_id=1, source_target_pairs={{0,2},{1,3},{2,4},{3,5},{4,6},{5,7},{6,8},{7,9},{8,10},{9,11},{10,... | collective-permute-start | bytes 172040
  491.9 105.0 %collective-permute-start.23 = (f32[56,256]{1,0:T(8,128)}, f32[56,256]{1,0:T(8,128)}, u32[]{:S(2)}, u32[]{:S(2)}) collective-permute-start(f32[56,256]{1,0:T(8,128)} %get-tuple-element.15), channel_id=1, source_target_pairs={{0,3},{1,4},{2,5},{3,6},{4,7},{5,8},{6,9},{7,10},{8,11},{9,12},{10... | collective-permute-start | bytes 172040
  502.9 108.2 %collective-permute-start.24 = (f32[56,256]{1,0:T(8,128)}, f32[56,256]{1,0:T(8,128)}, u32[]{:S(2)}, u32[]{:S(2)}) collective-permute-start(f32[56,256]{1,0:T(8,128)} %get-tuple-element.15), channel_id=1, source_target_pairs={{0,4},{1,5},{2,6},{3,7},{4,8},{5,9},{6,10},{7,11},{8,12},{9,13},{1... | collective-permute-start | bytes 172040
  514.2 62.6 %collective-permute-start.25 = (f32[30,256]{1,0:T(8,128)}, f32[30,256]{1,0:T(8,128)}, u32[]{:S(2)}, u32[]{:S(2)}) collective-permute-start(f32[30,256]{1,0:T(8,128)} %slice.943), channel_id=1, source_target_pairs={{0,5},{1,6},{2,7},{3,8},{4,9},{5,10},{6,11},{7,12},{8,13},{9,14},{... | collective-permute-start | bytes 92168
  576.8 63.1 %collective-permute-start.16 = (f32[56,256]{1,0:T(8,128)S(1)}, f32[56,256]{1,0:T(8,128)S(1)}, u32[]{:S(2)}, u32[]{:S(2)}) collective-permute-start(f32[56,256]{1,0:T(8,128)S(1)} %copy-done.41), channel_id=1, source_target_pairs={{0,1},{1,2},{2,3},{3,4},{4,5},{5,6},{6,7},{7,8},{8,9},{9,10},{10,1... | collective-permute-start | bytes 172040
  579.9 59.9 %collective-permute-start.17 = (f32[56,256]{1,0:T(8,128)S(1)}, f32[56,256]{1,0:T(8,128)S(1)}, u32[]{:S(2)}, u32[]{:S(2)}) collective-permute-start(f32[56,256]{1,0:T(8,128)S(1)} %copy-done.41), channel_id=1, source_target_pairs={{0,2},{1,3},{2,4},{3,5},{4,6},{5,7},{6,8},{7,9},{8,10},{9,11},{10,... | collective-permute-start | bytes 172040
  588.7 51.2 %collective-permute-start.18 = (f32[56,256]{1,0:T(8,128)S(1)}, f32[56,256]{1,0:T(8,128)S(1)}, u32[]{:S(2)}, u32[]{:S(2)}) collective-permute-start(f32[56,256]{1,0:T(8,128)S(1)} %copy-done.41), channel_id=1, source_target_pairs={{0,3},{1,4},{2,5},{3,6},{4,7},{5,8},{6,9},{7,10},{8,11},{9,12},{10... | collective-permute-start | bytes 172040
  596.9 43.0 %collective-permute-start.19 = (f32[56,256]{1,0:T(8,128)S(1)}, f32[56,256]{1,0:T(8,128)S(1)}, u32[]{:S(2)}, u32[]{:S(2)}) collective-permute-start(f32[56,256]{1,0:T(8,128)S(1)} %copy-done.41), channel_id=1, source_target_pairs={{0,4},{1,5},{2,6},{3,7},{4,8},{5,9},{6,10},{7,11},{8,12},{9,13},{1... | collective-permute-start | bytes 172040
  611.1 28.7 %collective-permute-start.20 = (f32[30,256]{1,0:T(8,128)}, f32[30,256]{1,0:T(8,128)S(1)}, u32[]{:S(2)}, u32[]{:S(2)}) collective-permute-start(f32[30,256]{1,0:T(8,128)} %slice.942), channel_id=1, source_target_pairs={{0,5},{1,6},{2,7},{3,8},{4,9},{5,10},{6,11},{7,12},{8,13},{9,14},{... | collective-permute-start | bytes 92168
  631.6 17.4 %all-to-all-start.1 = ((f32[16,54,256]{2,1,0:T(8,128)}), f32[16,54,256]{2,1,0:T(8,128)S(1)}, u32[]{:S(2)}, u32[]{:S(2)}) async-start(f32[16,54,256]{2,1,0:T(8,128)} %stack.263), calls=%async_computation.1 | async-start | bytes 1835008 | tf_op jit(solution)/shard_map/all_to_all | solution.py:74
  649.9 18.7 %all-to-all-start = ((f32[16,54,256]{2,1,0:T(8,128)}), f32[16,54,256]{2,1,0:T(8,128)S(1)}, u32[]{:S(2)}, u32[]{:S(2)}) async-start(f32[16,54,256]{2,1,0:T(8,128)} %stack.234), calls=%async_computation | async-start | bytes 1835008 | tf_op jit(solution)/shard_map/all_to_all | solution.py:74
  (51 other events, 330.2 us)
Sparse Core Ops, SparseCore 0:
  10.3 63.1 all-gather.2
  75.9 64.0 all-gather.4
